TPU v7x, 32 devices: a whole 2x2x4 slice. The times are simulated.
32 devices in a mesh: shard: 8 (over z, y), pair: 4 (over x, core).
Axes of the slice: x: 2, y: 2, z: 4, core: 2. Of those that a mesh axis runs over, the one named last changes fastest.
Arguments:
- embeds: float32 [8192, 768], P(('shard', 'pair')), may hold values from -256 to 256
- cluster: int32 [8192], P(('shard', 'pair')), may hold values from 0 to 127, as said below
- rank: int32 [8192], P(('shard', 'pair')), may hold values from 0 to 8191, each once
Outputs:
- best: float32 [8192], P(('shard', 'pair'))
Inputs may be any that keep to these rules, and one draw needn't show every extreme that they name: Among the rows of one device no group cluster // 16 is named more than 64 times and no quarter of a group more than 16 times; one group, the same for every device, is named exactly 64 times by the rows of every device, each of its quarters exactly 16 times. No two rows share a rank.
All inputs are finite; a program needn't handle non-finite values.
Results may differ from a plain program's by a relative error of at most 0.00031.
Values may be sent and summed in bfloat16 or wider, within the bound.
A program may use at most 64 MiB of HBM per device.

v0:
```python
import jax
import jax.numpy as jnp
from jax import lax
from jax.sharding import PartitionSpec as P

CL_OWN = 16


def from_behind(block, axis, distance):
    devices = range(lax.axis_size(axis))
    route = [((i - distance) % len(devices), i) for i in devices]
    return lax.ppermute(block, axis, route)


def compare(query_panel, key_panel, want_columns):
    query_units, query_clusters, query_ranks = query_panel
    key_units, key_clusters, key_ranks = key_panel
    query_rows = query_units.shape[0]
    tile_rows = min(512, query_rows)
    column_best = jnp.full((key_units.shape[0],), -1.0, jnp.float32)
    scores = jnp.einsum("qd,kd->qk", query_units, key_units, preferred_element_type=jnp.float32)
    same_cluster = query_clusters[0:tile_rows, None] == key_clusters[None, :]
    rank_here = query_ranks[0:tile_rows, None]
    earlier = key_ranks[None, :] < rank_here
    row_parts = jnp.max(jnp.where(same_cluster & earlier, scores, -1.0), axis=1)
    if want_columns:
        later_rank = rank_here < key_ranks[None, :]
        column_best = jnp.maximum(
            column_best, jnp.max(jnp.where(same_cluster & later_rank, scores, -1.0), axis=0)
        )
    return (row_parts, column_best)


def body(embeds, cluster, rank):
    local_rows = embeds.shape[0]
    width = embeds.shape[1]
    shard_count = lax.axis_size("shard")
    pair_count = lax.axis_size("pair")
    capacity = 2 * local_rows // shard_count
    sub_slots = capacity // pair_count
    slots = shard_count * capacity
    squares = jnp.sum(embeds * embeds, axis=1, keepdims=True)
    unit_rows = (embeds * lax.rsqrt(squares + 1e-06)).astype(jnp.bfloat16)
    home_group = cluster // CL_OWN
    quarter = cluster % CL_OWN * pair_count // CL_OWN
    bucket = home_group * pair_count + quarter
    row_index = jnp.arange(local_rows, dtype=jnp.int32)
    before = (bucket[:, None] == bucket[None, :]) & (row_index[None, :] < row_index[:, None])
    position = jnp.sum(before.astype(jnp.int32), axis=1)
    slot_index = home_group * capacity + quarter * sub_slots + position
    send_units = jnp.zeros((slots, width), jnp.bfloat16).at[slot_index].set(unit_rows)
    send_clusters = jnp.full((slots,), -1, jnp.int32).at[slot_index].set(cluster)
    send_ranks = jnp.zeros((slots,), jnp.int32).at[slot_index].set(rank)
    got_units, got_clusters, got_ranks = (
        lax.all_to_all(
            send_units.reshape(shard_count, capacity, width),
            "shard",
            split_axis=0,
            concat_axis=0,
            tiled=True,
        ),
        lax.all_to_all(
            send_clusters.reshape(shard_count, capacity),
            "shard",
            split_axis=0,
            concat_axis=0,
            tiled=True,
        ),
        lax.all_to_all(
            send_ranks.reshape(shard_count, capacity),
            "shard",
            split_axis=0,
            concat_axis=0,
            tiled=True,
        ),
    )
    own_panel = (
        got_units.reshape(slots, width),
        got_clusters.reshape(slots),
        got_ranks.reshape(slots),
    )
    best_slot, unused = compare(own_panel, own_panel, False)
    for offset in range(1, pair_count // 2 + 1):
        other_panel = from_behind((own_panel[0], own_panel[1], own_panel[2]), "pair", offset)
        both_sides = 2 * offset != pair_count
        found, column_best = compare(own_panel, other_panel, both_sides)
        best_slot = jnp.maximum(best_slot, found)
        if both_sides:
            returned = from_behind(column_best, "pair", pair_count - offset)
            best_slot = jnp.maximum(best_slot, returned)
    homeward = lax.all_to_all(
        best_slot.reshape(shard_count, capacity), "shard", split_axis=0, concat_axis=0, tiled=True
    )
    return homeward.reshape(slots)[slot_index]


def solution(mesh):
    in_specs = (P(("shard", "pair"), None), P(("shard", "pair")), P(("shard", "pair")))
    out_specs = P(("shard", "pair"))
    return jax.shard_map(body, mesh=mesh, in_specs=in_specs, out_specs=out_specs, check_vma=False)
```

profile of v0, /device:TPU:0, one launch (start us, length us, event | category | flops | bytes accessed | tf_op | source)
XLA Modules:
  0.0 77.3 jit_solution(13814901502001202132)
XLA Ops:
  0.0 0.8 multiply_add_fusion
  1.0 1.3 %multiply_reduce_fusion = f32[256]{0:T(256)S(1)} fusion(f32[256,768]{1,0:T(8,128)} %param.3), kind=kLoop, calls=%fused_computation.12 | loop fusion | flops 392960 | bytes 787456 | tf_op jit(solution)/shard_map/reduce_sum | solution.py:42
  2.3 2.0 %scatter_custom_fusion.2 = bf16[512,768]{1,0:T(8,128)(2,1)S(1)} fusion(s32[256]{0:T(256)S(1)} %compare_select_fusion, f32[256,768]{1,0:T(8,128)S(1)} %copy-done, f32[256]{0:T(256)S(1)} %add_rsqrt_fusion, bf16[]{:T(256)} %constant.51.clone.1), kind=kCustom, calls=%fused_computation.13 | custom fusion | flops 393216 | bytes 1573890 | tf_op jit(solution)/shard_map/scatter | solution.py:51
  4.2 27.3 %all_to_all.32 = bf16[8,64,768]{2,1,0:T(8,128)(2,1)S(1)} all-to-all(bf16[8,64,768]{2,1,0:T(8,128)(2,1)S(1)} %bitcast.8), channel_id=1, replica_groups=mesh['shard'=8,'pair'=4] {'shard'}, dimensions={0} | all-to-all | bytes 1572864 | tf_op jit(solution)/shard_map/all_to_all | solution.py:55
  31.5 1.5 %collective-permute-start.6 = (bf16[512,768]{1,0:T(8,128)(2,1)S(1)}, bf16[512,768]{1,0:T(8,128)(2,1)S(1)}, u32[]{:S(2)}, u32[]{:S(2)}) collective-permute-start(bf16[512,768]{1,0:T(8,128)(2,1)S(1)} %bitcast.9), channel_id=1, source_target_pairs={{2,0},{3,1},{0,2},{1,3},{6,4},{7,5},{4,6},{5,7},{10,8},{11,9},{8,1... | collective-permute-start | bytes 2359304 | tf_op jit(solution)/shard_map/ppermute | solution.py:12
  33.0 1.6 %scatter_custom_fusion.1 = s32[512]{0:T(512)S(1)} fusion(s32[256]{0:T(256)S(1)} %compare_select_fusion, s32[256]{0:T(256)} %param.5, s32[]{:T(128)} %constant.45.clone.1), kind=kCustom, calls=%fused_computation.34 | custom fusion | bytes 2560 | tf_op jit(solution)/shard_map/scatter | solution.py:53
  34.5 0.7 all_to_all.23
  35.2 3.6 %all-to-all-start.1 = ((s32[8,1,64]{2,1,0:T(1,128)}), s32[8,1,64]{2,1,0:T(1,128)S(1)}, u32[]{:S(2)}, u32[]{:S(2)}) async-start(s32[8,1,64]{2,1,0:T(1,128)} %all_to_all.23), calls=%async_computation.1 | async-start | bytes 8192 | tf_op jit(solution)/shard_map/all_to_all | solution.py:69
  38.8 1.6 %scatter_custom_fusion = s32[512]{0:T(512)S(1)} fusion(s32[256]{0:T(256)S(1)} %compare_select_fusion, s32[256]{0:T(256)} %param.4, s32[]{:T(128)} %constant.43.clone.1), kind=kCustom, calls=%fused_computation.37 | custom fusion | bytes 2560 | tf_op jit(solution)/shard_map/scatter | solution.py:52
  40.4 0.7 all_to_all.21
  41.0 4.3 %all-to-all-done.1 = s32[8,1,64]{2,1,0:T(1,128)S(1)} async-done(((s32[8,1,64]{2,1,0:T(1,128)}), s32[8,1,64]{2,1,0:T(1,128)S(1)}, u32[]{:S(2)}, u32[]{:S(2)}) %all-to-all-start.1) | async-done | bytes 2080 | tf_op jit(solution)/shard_map/all_to_all | solution.py:69
  45.3 3.2 %all-to-all-start = ((s32[8,1,64]{2,1,0:T(1,128)}), s32[8,1,64]{2,1,0:T(1,128)S(1)}, u32[]{:S(2)}, u32[]{:S(2)}) async-start(s32[8,1,64]{2,1,0:T(1,128)} %all_to_all.21), calls=%async_computation | async-start | bytes 8192 | tf_op jit(solution)/shard_map/all_to_all | solution.py:62
  49.1 0.7 reduce.9
  49.8 0.7 collective-permute-start.5
  50.5 4.5 %all-to-all-done = s32[8,1,64]{2,1,0:T(1,128)S(1)} async-done(((s32[8,1,64]{2,1,0:T(1,128)}), s32[8,1,64]{2,1,0:T(1,128)S(1)}, u32[]{:S(2)}, u32[]{:S(2)}) %all-to-all-start) | async-done | bytes 2080 | tf_op jit(solution)/shard_map/all_to_all | solution.py:62
  55.0 0.7 reduce.10
  56.9 1.8 %collective-permute-done = s32[512]{0:T(512)S(1)} collective-permute-done((s32[512]{0:T(512)S(1)}, s32[512]{0:T(512)S(1)}, u32[]{:S(2)}, u32[]{:S(2)}) %collective-permute-start) | collective-permute-done | bytes 2080 | tf_op jit(solution)/shard_map/ppermute | solution.py:12
  59.4 1.3 %select_reduce_fusion.2 = (f32[512]{0:T(512)S(1)}, f32[512]{0:T(512)S(1)}, f32[512]{0:T(512)S(1)}) fusion(s32[512]{0:T(512)S(1)} %lt.37, s32[512]{0:T(512)S(1)} %eq.27, s32[512]{0:T(512)S(1)} %collective-permute-done, s32[512]{0:T(512)S(1)} %collective-permute-done.1, f32[512,512]{0,1:T(8,128)S(1)} %fusion.10, s32[512]{0:T(512)S(1)} %collective-permute-done.5, ...), kind=kOutput, calls=%fused_computation.10 | convolution fusion | flops 406321664 | bytes 2639872 | tf_op jit(solution)/shard_map/qd,kd->qk/dot_general | solution.py:21
  61.9 0.7 collective-permute-done.3
  62.6 0.7 all_to_all.26
  63.2 3.8 %all-to-all-start.3 = ((f32[8,1,64]{2,1,0:T(1,128)}), f32[8,1,64]{2,1,0:T(1,128)S(1)}, u32[]{:S(2)}, u32[]{:S(2)}) async-start(f32[8,1,64]{2,1,0:T(1,128)} %all_to_all.26), calls=%async_computation.3 | async-start | bytes 8192 | tf_op jit(solution)/shard_map/all_to_all | solution.py:91
  67.1 6.5 %all-to-all-done.3 = f32[8,1,64]{2,1,0:T(1,128)S(1)} async-done(((f32[8,1,64]{2,1,0:T(1,128)}), f32[8,1,64]{2,1,0:T(1,128)S(1)}, u32[]{:S(2)}, u32[]{:S(2)}) %all-to-all-start.3) | async-done | bytes 2080 | tf_op jit(solution)/shard_map/all_to_all | solution.py:91
  74.1 0.7 reduce.11
  74.8 2.5 %gather_fusion = f32[256]{0:T(256)} fusion(f32[512]{0:T(512)S(1)} %reshape.48, s32[1024]{0:T(1024)S(1)} %pad_clamp_fusion), kind=kCustom, calls=%fused_computation | custom fusion | bytes 3072 | tf_op jit(solution)/shard_map/gather | solution.py:94
  (25 shorter events, 4.5 us)
Async XLA Ops:
  0.0 2.2 %copy-start = (f32[256,768]{1,0:T(8,128)S(1)}, f32[256,768]{1,0:T(8,128)}, u32[]{:S(2)}) copy-start(f32[256,768]{1,0:T(8,128)} %param.3) | copy-start | bytes 2359300
  31.5 24.2 %collective-permute-start.6 = (bf16[512,768]{1,0:T(8,128)(2,1)S(1)}, bf16[512,768]{1,0:T(8,128)(2,1)S(1)}, u32[]{:S(2)}, u32[]{:S(2)}) collective-permute-start(bf16[512,768]{1,0:T(8,128)(2,1)S(1)} %bitcast.9), channel_id=1, source_target_pairs={{2,0},{3,1},{0,2},{1,3},{6,4},{7,5},{4,6},{5,7},{10,8},{11,9},{8,1... | collective-permute-start | bytes 2359304 | tf_op jit(solution)/shard_map/ppermute | solution.py:12
  33.0 26.4 %collective-permute-start.2 = (bf16[512,768]{1,0:T(8,128)(2,1)S(1)}, bf16[512,768]{1,0:T(8,128)(2,1)S(1)}, u32[]{:S(2)}, u32[]{:S(2)}) collective-permute-start(bf16[512,768]{1,0:T(8,128)(2,1)S(1)} %bitcast.10), channel_id=1, source_target_pairs={{3,0},{0,1},{1,2},{2,3},{7,4},{4,5},{5,6},{6,7},{11,8},{8,9},{9,10... | collective-permute-start | bytes 2359304 | tf_op jit(solution)/shard_map/ppermute | solution.py:12
  35.2 10.1 %all-to-all-start.1 = ((s32[8,1,64]{2,1,0:T(1,128)}), s32[8,1,64]{2,1,0:T(1,128)S(1)}, u32[]{:S(2)}, u32[]{:S(2)}) async-start(s32[8,1,64]{2,1,0:T(1,128)} %all_to_all.23), calls=%async_computation.1 | async-start | bytes 8192 | tf_op jit(solution)/shard_map/all_to_all | solution.py:69
  45.3 9.7 %all-to-all-start = ((s32[8,1,64]{2,1,0:T(1,128)}), s32[8,1,64]{2,1,0:T(1,128)S(1)}, u32[]{:S(2)}, u32[]{:S(2)}) async-start(s32[8,1,64]{2,1,0:T(1,128)} %all_to_all.21), calls=%async_computation | async-start | bytes 8192 | tf_op jit(solution)/shard_map/all_to_all | solution.py:62
  49.8 8.9 %collective-permute-start.1 = (s32[512]{0:T(512)S(1)}, s32[512]{0:T(512)S(1)}, u32[]{:S(2)}, u32[]{:S(2)}) collective-permute-start(s32[512]{0:T(512)S(1)} %lt.37), channel_id=1, source_target_pairs={{3,0},{0,1},{1,2},{2,3},{7,4},{4,5},{5,6},{6,7},{11,8},{8,9},{9,10... | collective-permute-start | bytes 6152 | tf_op jit(solution)/shard_map/ppermute | solution.py:12
  49.8 8.9 %collective-permute-start.5 = (s32[512]{0:T(512)S(1)}, s32[512]{0:T(512)S(1)}, u32[]{:S(2)}, u32[]{:S(2)}) collective-permute-start(s32[512]{0:T(512)S(1)} %lt.37), channel_id=1, source_target_pairs={{2,0},{3,1},{0,2},{1,3},{6,4},{7,5},{4,6},{5,7},{10,8},{11,9},{8,1... | collective-permute-start | bytes 6152 | tf_op jit(solution)/shard_map/ppermute | solution.py:12
  55.7 3.0 %collective-permute-start = (s32[512]{0:T(512)S(1)}, s32[512]{0:T(512)S(1)}, u32[]{:S(2)}, u32[]{:S(2)}) collective-permute-start(s32[512]{0:T(512)S(1)} %eq.27), channel_id=1, source_target_pairs={{3,0},{0,1},{1,2},{2,3},{7,4},{4,5},{5,6},{6,7},{11,8},{8,9},{9,10... | collective-permute-start | bytes 6152 | tf_op jit(solution)/shard_map/ppermute | solution.py:12
  55.7 3.7 %collective-permute-start.4 = (s32[512]{0:T(512)S(1)}, s32[512]{0:T(512)S(1)}, u32[]{:S(2)}, u32[]{:S(2)}) collective-permute-start(s32[512]{0:T(512)S(1)} %eq.27), channel_id=1, source_target_pairs={{2,0},{3,1},{0,2},{1,3},{6,4},{7,5},{4,6},{5,7},{10,8},{11,9},{8,1... | collective-permute-start | bytes 6152 | tf_op jit(solution)/shard_map/ppermute | solution.py:12
  60.7 1.9 %collective-permute-start.3 = (f32[512]{0:T(512)S(1)}, f32[512]{0:T(512)S(1)}, u32[]{:S(2)}, u32[]{:S(2)}) collective-permute-start(f32[512]{0:T(512)S(1)} %broadcast_maximum_fusion), channel_id=1, source_target_pairs={{1,0},{2,1},{3,2},{0,3},{5,4},{6,5},{7,6},{4,7},{9,8},{10,9},{11,1... | collective-permute-start | bytes 6152 | tf_op jit(solution)/shard_map/ppermute | solution.py:12
  63.2 10.3 %all-to-all-start.3 = ((f32[8,1,64]{2,1,0:T(1,128)}), f32[8,1,64]{2,1,0:T(1,128)S(1)}, u32[]{:S(2)}, u32[]{:S(2)}) async-start(f32[8,1,64]{2,1,0:T(1,128)} %all_to_all.26), calls=%async_computation.3 | async-start | bytes 8192 | tf_op jit(solution)/shard_map/all_to_all | solution.py:91
where the time goes:
time: 77.7 us; the launch traced here: 77.3 us
  blocking collectives  27.3 us (35%)
  waiting for transfers between devices  18.3 us (24%)
  starting transfers between devices  14.1 us (18%)
  local copies, waits for them, and re-layouts  8.88 us (11%)
  other arithmetic  6.18 us (8%)
  matrix products  2.53 us (3%)
    all_to_all x1, blocking collectives, body(): lax.all_to_all(send_units.reshape(shard_count, capacity, width), 'shard',...  27.3 us
    all_to_all x1, waiting for transfers between devices, body(): lax.all_to_all(best_slot.reshape(shard_count, capacity), 'shard', split_a...  6.49 us
    all_to_all x1, waiting for transfers between devices, body(): lax.all_to_all(send_clusters.reshape(shard_count, capacity), 'shard', spl...  4.46 us
    all_to_all x1, waiting for transfers between devices, body(): lax.all_to_all(send_ranks.reshape(shard_count, capacity), 'shard', split_...  4.27 us
    all_to_all x1, starting transfers between devices, body(): lax.all_to_all(best_slot.reshape(shard_count, capacity), 'shard', split_a...  3.85 us
    all_to_all x1, starting transfers between devices, body(): lax.all_to_all(send_ranks.reshape(shard_count, capacity), 'shard', split_...  3.59 us
    ppermute x7, starting transfers between devices, from_behind(): return lax.ppermute(block, axis, route)  3.36 us
    all_to_all x1, starting transfers between devices, body(): lax.all_to_all(send_clusters.reshape(shard_count, capacity), 'shard', spl...  3.25 us
  transfers between devices with their start and end apart: 10, of which 6 were waited for; matrix products, arithmetic and copies ran while one was open for 8% of the time, Pallas kernels for 0%

commit v1 on v0

v1 whole, which is shorter than its diff:
```python
import functools

import jax
import jax.numpy as jnp
from jax import lax
from jax.experimental import pallas as pl
from jax.experimental.pallas import tpu as pltpu
from jax.sharding import PartitionSpec as P

CL_OWN = 16
LANES = 128
MESH = pl.DeviceIdType.MESH


def log2(value):
    return (value - 1).bit_length()


def kernel(
    pairs, sub, bits, step_bits,
    embeds_ref, cluster_ref, rank_ref, out_ref,
    send_u, recv_u, send_k, recv_k, answers, returned,
    u_send, u_recv, k_send, k_recv, a_send, a_recv,
):
    devices = recv_u.shape[0]
    rows, width = embeds_ref.shape
    slots = devices * sub
    per = LANES // sub
    chunks = devices // per
    me = lax.axis_index("shard") * pairs + lax.axis_index("pair")
    my_chunk = me // per
    my_place = me % per

    def coords(device):
        return (device // pairs, device % pairs)

    def copy_units(device):
        return pltpu.make_async_remote_copy(
            src_ref=send_u.at[device], dst_ref=recv_u.at[me],
            send_sem=u_send.at[device], recv_sem=u_recv.at[me],
            device_id=coords(device), device_id_type=MESH)

    def copy_keys(device):
        return pltpu.make_async_remote_copy(
            src_ref=send_k.at[device // per], dst_ref=recv_k.at[me],
            send_sem=k_send.at[device], recv_sem=k_recv.at[me],
            device_id=coords(device), device_id_type=MESH)

    def copy_answers(device):
        return pltpu.make_async_remote_copy(
            src_ref=answers.at[device // per], dst_ref=returned.at[me],
            send_sem=a_send.at[device], recv_sem=a_recv.at[me],
            device_id=coords(device), device_id_type=MESH)

    def await_from(device):
        def wait(buffer, send, recv):
            pltpu.make_async_remote_copy(
                src_ref=buffer.at[device], dst_ref=buffer.at[device],
                send_sem=send.at[device], recv_sem=recv.at[device],
                device_id=coords(device), device_id_type=MESH).wait_recv()
        return wait

    def others(action):
        def step(k, carry):
            action(lax.rem(me + k, devices))
            return carry
        lax.fori_loop(1, devices, step, 0)

    if chunks == 4:
        order = [3 - my_chunk, (my_chunk + 2) % 4, my_chunk + 1 - 2 * (my_chunk % 2), my_chunk]
    else:
        order = [(my_chunk + chunks // 2 + k) % chunks for k in range(chunks)]
        order = [c for c in order]

    barrier = pltpu.get_barrier_semaphore()
    others(lambda d: pl.semaphore_signal(barrier, inc=1, device_id=coords(d), device_id_type=MESH))

    cluster = cluster_ref[...]
    key = cluster * (1 << bits) + rank_ref[...]
    bucket = lax.shift_right_logical(cluster, step_bits)

    def columns(row):
        return jnp.transpose(jnp.broadcast_to(row, (LANES, row.shape[1])))

    bucket_column = columns(bucket)
    lower = lax.broadcasted_iota(jnp.int32, (rows, LANES), 0)
    lane = lax.broadcasted_iota(jnp.int32, (rows, LANES), 1)
    places = []
    for part in range(rows // LANES):
        here = bucket[:, part * LANES:(part + 1) * LANES]
        before = (bucket_column == here) & (lower < lane + part * LANES)
        places.append(jnp.sum(before.astype(jnp.int32), axis=0, keepdims=True))
    position = jnp.concatenate(places, axis=1)
    slot = bucket * sub + position
    slot_column = columns(slot)
    key_column = columns(key)
    for part in range(chunks):
        found = jnp.where(slot_column == lane + part * LANES, key_column, -1)
        send_k[part] = jnp.max(found, axis=0, keepdims=True)

    embeds = embeds_ref[...]
    squares = jnp.sum(embeds * embeds, axis=1, keepdims=True)
    unit = (embeds * lax.rsqrt(squares + 1e-06)).astype(jnp.bfloat16)
    chunk_row = lax.broadcasted_iota(jnp.int32, (LANES, rows), 0)

    for index, chunk in enumerate(order):
        pick = (slot == chunk_row + chunk * LANES).astype(jnp.float32).astype(jnp.bfloat16)
        placed = jnp.dot(pick, unit, preferred_element_type=jnp.float32).astype(jnp.bfloat16)
        send_u[pl.ds(chunk * per, per)] = placed.reshape(per, sub, width)
        if index == 0:
            pl.semaphore_wait(barrier, devices - 1)

        def launch(k, carry, chunk=chunk):
            device = chunk * per + lax.rem(my_place + k, per)
            copy_keys(device).start()
            copy_units(device).start()
            return carry

        lax.fori_loop(1 if index == chunks - 1 else 0, per, launch, 0)

    recv_u[me] = send_u[me]
    recv_k[me] = send_k[my_chunk]

    others(lambda d: await_from(d)(recv_k, k_send, k_recv))
    offset = my_place * sub
    key_rows = []
    place_lane = lax.broadcasted_iota(jnp.int32, (per, LANES), 1)
    place_row = lax.broadcasted_iota(jnp.int32, (per, LANES), 0)
    in_place = (place_lane >= place_row * sub) & (place_lane < place_row * sub + sub)
    for part in range(chunks):
        block = recv_k[part * per:(part + 1) * per].reshape(per, LANES)
        block = pltpu.roll(pltpu.roll(block, lax.rem(LANES - offset, LANES), 1), 0, 1, stride=sub, stride_axis=0)
        key_rows.append(jnp.max(jnp.where(in_place, block, -1), axis=0, keepdims=True))
    keys = jnp.concatenate(key_rows, axis=1)
    keys_column = columns(keys)

    others(lambda d: await_from(d)(recv_u, u_send, u_recv))
    panel = recv_u[...].reshape(slots, width)
    for index, chunk in enumerate(order):
        queries = recv_u[pl.ds(chunk * per, per)].reshape(LANES, width)
        scores = lax.dot_general(panel, queries, (((1,), (1,)), ((), ())), preferred_element_type=jnp.float32)
        query_keys = jnp.full((1, LANES), -1, jnp.int32)
        for part in range(chunks):
            query_keys = jnp.where(chunk == part, key_rows[part], query_keys)
        first = query_keys & (-(1 << bits))
        mask = (keys_column < query_keys) & (keys_column >= first)
        answers[chunk] = jnp.max(jnp.where(mask, scores, -1.0), axis=0, keepdims=True)

        def answer(k, carry, chunk=chunk):
            copy_answers(chunk * per + lax.rem(my_place + k, per)).start()
            return carry

        lax.fori_loop(1 if index == chunks - 1 else 0, per, answer, 0)

    returned[me] = answers[my_chunk]
    others(lambda d: await_from(d)(returned, a_send, a_recv))
    gathered = returned[...].reshape(devices, LANES)
    device_row = lax.broadcasted_iota(jnp.int32, (devices, rows), 0)
    from_bucket = (device_row == bucket).astype(jnp.float32)
    spread = lax.dot_general(
        gathered, from_bucket, (((0,), (0,)), ((), ())),
        precision=lax.Precision.HIGHEST, preferred_element_type=jnp.float32)
    want = position + offset
    out_ref[...] = jnp.sum(jnp.where(chunk_row == want, spread, 0.0), axis=0, keepdims=True)

    def finish(d):
        copy_keys(d).wait_send()
        copy_units(d).wait_send()
        copy_answers(d).wait_send()

    others(finish)


def kernel_body(shards, pairs, embeds, cluster, rank):
    rows, width = embeds.shape
    devices = shards * pairs
    sub = 2 * rows // devices
    bits = log2(devices * rows)
    per = LANES // sub
    chunks = devices // per
    vmem = pl.BlockSpec(memory_space=pltpu.VMEM)
    best = pl.pallas_call(
        functools.partial(kernel, pairs, sub, bits, log2(CL_OWN // pairs)),
        out_shape=jax.ShapeDtypeStruct((1, rows), jnp.float32),
        in_specs=[vmem] * 3,
        out_specs=vmem,
        scratch_shapes=[
            pltpu.VMEM((devices, sub, width), jnp.bfloat16),
            pltpu.VMEM((devices, sub, width), jnp.bfloat16),
            pltpu.VMEM((chunks, 1, LANES), jnp.int32),
            pltpu.VMEM((devices, 1, LANES), jnp.int32),
            pltpu.VMEM((chunks, 1, LANES), jnp.float32),
            pltpu.VMEM((devices, 1, LANES), jnp.float32),
        ] + [pltpu.SemaphoreType.DMA((devices,))] * 6,
        compiler_params=pltpu.CompilerParams(collective_id=0, has_side_effects=True),
    )(embeds, cluster.reshape(1, rows), rank.reshape(1, rows))
    return best.reshape(rows)


def plain_body(embeds, cluster, rank):
    rows, width = embeds.shape
    pairs = lax.axis_size("pair")
    devices = lax.axis_size("shard") * pairs
    sub = 2 * rows // devices
    slots = devices * sub
    squares = jnp.sum(embeds * embeds, axis=1, keepdims=True)
    unit_rows = (embeds * lax.rsqrt(squares + 1e-06)).astype(jnp.bfloat16)
    bucket = cluster // CL_OWN * pairs + cluster % CL_OWN * pairs // CL_OWN
    index = jnp.arange(rows, dtype=jnp.int32)
    before = (bucket[:, None] == bucket[None, :]) & (index[None, :] < index[:, None])
    slot = bucket * sub + jnp.sum(before.astype(jnp.int32), axis=1)

    def exchange(array):
        blocks = array.reshape((devices, sub) + array.shape[1:])
        return lax.all_to_all(blocks, ("shard", "pair"), 0, 0, tiled=True).reshape(array.shape)

    units = exchange(jnp.zeros((slots, width), jnp.bfloat16).at[slot].set(unit_rows))
    clusters = exchange(jnp.full((slots,), -1, jnp.int32).at[slot].set(cluster))
    ranks = exchange(jnp.zeros((slots,), jnp.int32).at[slot].set(rank))
    scores = jnp.einsum("qd,kd->qk", units, units, preferred_element_type=jnp.float32)
    mask = (clusters[:, None] == clusters[None, :]) & (ranks[None, :] < ranks[:, None])
    return exchange(jnp.max(jnp.where(mask, scores, -1.0), axis=1))[slot]


def solution(mesh):
    shards, pairs = mesh.shape["shard"], mesh.shape["pair"]
    devices = shards * pairs

    def body(embeds, cluster, rank):
        rows, width = embeds.shape
        sub = 2 * rows // devices
        quarter = CL_OWN // pairs
        fits = (
            CL_OWN % pairs == 0 and quarter & (quarter - 1) == 0
            and sub % 16 == 0 and LANES % sub == 0 and devices % (LANES // sub) == 0
            and rows % LANES == 0 and width % LANES == 0
        )
        if fits:
            return kernel_body(shards, pairs, embeds, cluster, rank)
        return plain_body(embeds, cluster, rank)

    in_specs = (P(("shard", "pair"), None), P(("shard", "pair")), P(("shard", "pair")))
    return jax.shard_map(body, mesh=mesh, in_specs=in_specs, out_specs=P(("shard", "pair")), check_vma=False)
```

time: 77.7 us -> 37.9 us (0.49)
  Pallas kernels: 0 us -> 36.5 us
  blocking collectives: 27.3 us -> 0 us
  waiting for transfers between devices: 18.3 us -> 0 us
  starting transfers between devices: 14.1 us -> 0 us
  local copies, waits for them, and re-layouts: 8.88 us -> 1.22 us
  other arithmetic: 6.18 us -> 0 us
  matrix products: 2.53 us -> 0 us
    pallas_call x0 -> x1, Pallas kernels: none -> 36.5 us  [kernel_body(): pl.pallas_call(functools.partial(kernel, pairs, sub, bits, log2(CL_OWN //...]
    all_to_all x1 -> x0, blocking collectives: 27.3 us -> none  [body(): lax.all_to_all(send_units.reshape(shard_count, capacity, width), 'shard',...]
    all_to_all x3 -> x0, waiting for transfers between devices: 15.2 us -> none  [the longest x1 6.49 us: body(): lax.all_to_all(best_slot.reshape(shard_count, capacity), 'shard', split_a...]
    all_to_all x3 -> x0, starting transfers between devices: 10.7 us -> none  [the longest x1 3.85 us: body(): lax.all_to_all(best_slot.reshape(shard_count, capacity), 'shard', split_a...]
    ppermute x7 -> x0, starting transfers between devices: 3.36 us -> none  [from_behind(): return lax.ppermute(block, axis, route)]
    ppermute x7 -> x0, waiting for transfers between devices: 3.11 us -> none  [from_behind(): return lax.ppermute(block, axis, route)]
    scatter x2 -> x0, local copies, waits for them, and re-layouts: 3.1 us -> none  [the longest x1 1.55 us: body(): send_ranks = jnp.zeros((slots,), jnp.int32).at[slot_index].set(rank)]
    all_to_all x5 -> x0, local copies, waits for them, and re-layouts: 3.04 us -> none  [the longest x2 1.19 us: body(): lax.all_to_all(send_ranks.reshape(shard_count, capacity), 'shard', split_...]
  transfers between devices with their start and end apart: 10 -> 0, of which waited for: 6 -> 0; matrix products, arithmetic and copies ran while one was open for 8% -> 0% of each run, Pallas kernels for 0% -> 0%
where the time goes in v1:
time: 37.9 us; the launch traced here: 37.8 us
  Pallas kernels  36.5 us (96%)
  local copies, waits for them, and re-layouts  1.22 us (3%)
    pallas_call x1, Pallas kernels, kernel_body(): pl.pallas_call(functools.partial(kernel, pairs, sub, bits, log2(CL_OWN //...  36.5 us
    unnamed x3, local copies, waits for them, and re-layouts  1.22 us

profile of v1, /device:TPU:0, one launch (start us, length us, event | category | flops | bytes accessed | tf_op | source)
XLA Modules:
  0.0 37.8 jit_solution(13503587122265205685)
XLA Ops:
  0.0 36.5 %shard_map.37 = f32[1,256]{1,0:T(1,128)} custom-call(f32[256,768]{1,0:T(8,128)} %embeds_ref.1, s32[1,256]{1,0:T(1,128)} %bitcast.4, s32[1,256]{1,0:T(1,128)} %bitcast.5), custom_call_target="tpu_custom_call" | custom-call | tf_op jit(solution)/shard_map/pallas_call | solution.py:182
  36.6 0.0 copy-start
  36.6 0.7 %copy-done = f32[1,256]{1,0:T(1,128)S(1)} copy-done((f32[1,256]{1,0:T(1,128)S(1)}, f32[1,256]{1,0:T(1,128)}, u32[]{:S(2)}) %copy-start) | copy-done | bytes 1048
  37.2 0.6 %copy.5 = f32[256]{0:T(256)} copy(f32[256]{0:T(256)S(1)} %bitcast.3) | data formatting | bytes 2048
Async XLA Ops:
  36.6 0.7 %copy-start = (f32[1,256]{1,0:T(1,128)S(1)}, f32[1,256]{1,0:T(1,128)}, u32[]{:S(2)}) copy-start(f32[1,256]{1,0:T(1,128)} %shard_map.37) | copy-start | bytes 3076

commit v2 on v1

--- a/solution.py
+++ b/solution.py
@@ -18,9 +18,10 @@
 
 def kernel(
     pairs, sub, bits, step_bits,
-    embeds_ref, cluster_ref, rank_ref, out_ref,
+    embeds_in, cluster_in, rank_in, out_ref,
+    embeds_ref, cluster_ref, rank_ref,
     send_u, recv_u, send_k, recv_k, answers, returned,
-    u_send, u_recv, k_send, k_recv, a_send, a_recv,
+    u_send, u_recv, k_send, k_recv, a_send, a_recv, in_sems, complete,
 ):
     devices = recv_u.shape[0]
     rows, width = embeds_ref.shape
@@ -70,11 +71,39 @@
         order = [3 - my_chunk, (my_chunk + 2) % 4, my_chunk + 1 - 2 * (my_chunk % 2), my_chunk]
     else:
         order = [(my_chunk + chunks // 2 + k) % chunks for k in range(chunks)]
-        order = [c for c in order]
 
     barrier = pltpu.get_barrier_semaphore()
-    others(lambda d: pl.semaphore_signal(barrier, inc=1, device_id=coords(d), device_id_type=MESH))
-
+    line, side = my_place // 2, my_place % 2
+    lines = per // 2
+
+    def on_line(k):
+        spot = lax.rem(my_chunk * 2 + side + k, 2 * chunks)
+        return (spot // 2) * per + line * 2 + spot % 2
+
+    def beside(k):
+        return my_chunk * per + lax.rem(line + k, lines) * 2 + side
+
+    def signal(semaphore, device):
+        pl.semaphore_signal(semaphore, inc=1, device_id=coords(device), device_id_type=MESH)
+
+    def run(start, stop, action):
+        def step(k, carry):
+            action(k)
+            return carry
+        lax.fori_loop(start, stop, step, 0)
+
+    run(1, 2 * chunks, lambda k: signal(barrier, on_line(k)))
+    run(1, lines, lambda k: signal(barrier, beside(k)))
+
+    loads = [
+        pltpu.make_async_copy(source, target, in_sems.at[k])
+        for k, (source, target) in enumerate(
+            [(cluster_in, cluster_ref), (rank_in, rank_ref), (embeds_in, embeds_ref)])
+    ]
+    for load in loads:
+        load.start()
+    loads[0].wait()
+    loads[1].wait()
     cluster = cluster_ref[...]
     key = cluster * (1 << bits) + rank_ref[...]
     bucket = lax.shift_right_logical(cluster, step_bits)
@@ -98,25 +127,35 @@
         found = jnp.where(slot_column == lane + part * LANES, key_column, -1)
         send_k[part] = jnp.max(found, axis=0, keepdims=True)
 
+    loads[2].wait()
     embeds = embeds_ref[...]
     squares = jnp.sum(embeds * embeds, axis=1, keepdims=True)
     unit = (embeds * lax.rsqrt(squares + 1e-06)).astype(jnp.bfloat16)
     chunk_row = lax.broadcasted_iota(jnp.int32, (LANES, rows), 0)
 
-    for index, chunk in enumerate(order):
+    def send(device):
+        copy_keys(device).start()
+        copy_units(device).start()
+
+    def place(chunk):
         pick = (slot == chunk_row + chunk * LANES).astype(jnp.float32).astype(jnp.bfloat16)
         placed = jnp.dot(pick, unit, preferred_element_type=jnp.float32).astype(jnp.bfloat16)
         send_u[pl.ds(chunk * per, per)] = placed.reshape(per, sub, width)
-        if index == 0:
-            pl.semaphore_wait(barrier, devices - 1)
-
-        def launch(k, carry, chunk=chunk):
-            device = chunk * per + lax.rem(my_place + k, per)
-            copy_keys(device).start()
-            copy_units(device).start()
-            return carry
-
-        lax.fori_loop(1 if index == chunks - 1 else 0, per, launch, 0)
+
+    early = chunks // 2
+    for chunk in order[:early]:
+        place(chunk)
+    pl.semaphore_wait(barrier, 2 * chunks - 1 + lines - 1)
+    run(1, lines, lambda k: signal(complete, beside(k)))
+    for chunk in order[:early]:
+        run(0, 2, lambda k, chunk=chunk: send(chunk * per + line * 2 + lax.rem(side + k, 2)))
+    for chunk in order[early:]:
+        place(chunk)
+    pl.semaphore_wait(complete, lines - 1)
+    for index, chunk in enumerate(order):
+        first = 2 if index < early else 1 if index == chunks - 1 else 0
+        base = my_place if index == chunks - 1 else line * 2
+        run(first, per, lambda k, chunk=chunk, base=base: send(chunk * per + lax.rem(base + k, per)))
 
     recv_u[me] = send_u[me]
     recv_k[me] = send_k[my_chunk]
@@ -182,16 +221,20 @@
     best = pl.pallas_call(
         functools.partial(kernel, pairs, sub, bits, log2(CL_OWN // pairs)),
         out_shape=jax.ShapeDtypeStruct((1, rows), jnp.float32),
-        in_specs=[vmem] * 3,
+        in_specs=[pl.BlockSpec(memory_space=pl.ANY)] * 3,
         out_specs=vmem,
         scratch_shapes=[
+            pltpu.VMEM((rows, width), jnp.float32),
+            pltpu.VMEM((1, rows), jnp.int32),
+            pltpu.VMEM((1, rows), jnp.int32),
             pltpu.VMEM((devices, sub, width), jnp.bfloat16),
             pltpu.VMEM((devices, sub, width), jnp.bfloat16),
             pltpu.VMEM((chunks, 1, LANES), jnp.int32),
             pltpu.VMEM((devices, 1, LANES), jnp.int32),
             pltpu.VMEM((chunks, 1, LANES), jnp.float32),
             pltpu.VMEM((devices, 1, LANES), jnp.float32),
-        ] + [pltpu.SemaphoreType.DMA((devices,))] * 6,
+        ] + [pltpu.SemaphoreType.DMA((devices,))] * 6
+        + [pltpu.SemaphoreType.DMA((3,)), pltpu.SemaphoreType.REGULAR],
         compiler_params=pltpu.CompilerParams(collective_id=0, has_side_effects=True),
     )(embeds, cluster.reshape(1, rows), rank.reshape(1, rows))
     return best.reshape(rows)

time: 37.9 us -> 35.9 us (0.947)
  Pallas kernels: 36.5 us -> 34.5 us
    pallas_call x1, Pallas kernels: 36.5 us -> 34.5 us  [kernel_body(): pl.pallas_call(functools.partial(kernel, pairs, sub, bits, log2(CL_OWN //...]
where the time goes in v2:
time: 35.9 us; the launch traced here: 35.7 us
  Pallas kernels  34.5 us (96%)
  local copies, waits for them, and re-layouts  1.22 us (3%)
    pallas_call x1, Pallas kernels, kernel_body(): pl.pallas_call(functools.partial(kernel, pairs, sub, bits, log2(CL_OWN //...  34.5 us
    unnamed x3, local copies, waits for them, and re-layouts  1.22 us

profile of v2, /device:TPU:0, one launch (start us, length us, event | category | flops | bytes accessed | tf_op | source)
XLA Modules:
  0.0 35.7 jit_solution(3614279019846987657)
XLA Ops:
  0.0 34.5 %shard_map.37 = f32[1,256]{1,0:T(1,128)} custom-call(f32[256,768]{1,0:T(8,128)} %embeds_in.1, s32[1,256]{1,0:T(1,128)} %bitcast.4, s32[1,256]{1,0:T(1,128)} %bitcast.5), custom_call_target="tpu_custom_call" | custom-call | tf_op jit(solution)/shard_map/pallas_call | solution.py:221
  34.5 0.0 copy-start
  34.5 0.7 %copy-done = f32[1,256]{1,0:T(1,128)S(1)} copy-done((f32[1,256]{1,0:T(1,128)S(1)}, f32[1,256]{1,0:T(1,128)}, u32[]{:S(2)}) %copy-start) | copy-done | bytes 1048
  35.1 0.6 %copy.5 = f32[256]{0:T(256)} copy(f32[256]{0:T(256)S(1)} %bitcast.3) | data formatting | bytes 2048
Async XLA Ops:
  34.5 0.7 %copy-start = (f32[1,256]{1,0:T(1,128)S(1)}, f32[1,256]{1,0:T(1,128)}, u32[]{:S(2)}) copy-start(f32[1,256]{1,0:T(1,128)} %shard_map.37) | copy-start | bytes 3076

commit v3 on v2

--- a/solution.py
+++ b/solution.py
@@ -67,10 +67,7 @@
             return carry
         lax.fori_loop(1, devices, step, 0)
 
-    if chunks == 4:
-        order = [3 - my_chunk, (my_chunk + 2) % 4, my_chunk + 1 - 2 * (my_chunk % 2), my_chunk]
-    else:
-        order = [(my_chunk + chunks // 2 + k) % chunks for k in range(chunks)]
+    order = [3 - my_chunk, (my_chunk + 2) % 4, my_chunk + 1 - 2 * (my_chunk % 2), my_chunk]
 
     barrier = pltpu.get_barrier_semaphore()
     line, side = my_place // 2, my_place % 2
@@ -170,28 +167,68 @@
         block = recv_k[part * per:(part + 1) * per].reshape(per, LANES)
         block = pltpu.roll(pltpu.roll(block, lax.rem(LANES - offset, LANES), 1), 0, 1, stride=sub, stride_axis=0)
         key_rows.append(jnp.max(jnp.where(in_place, block, -1), axis=0, keepdims=True))
-    keys = jnp.concatenate(key_rows, axis=1)
-    keys_column = columns(keys)
-
-    others(lambda d: await_from(d)(recv_u, u_send, u_recv))
-    panel = recv_u[...].reshape(slots, width)
-    for index, chunk in enumerate(order):
-        queries = recv_u[pl.ds(chunk * per, per)].reshape(LANES, width)
+
+    def await_units(chunk, mine):
+        def step(k, carry):
+            await_from(chunk * per + lax.rem(my_place + k, per))(recv_u, u_send, u_recv)
+            return carry
+        lax.fori_loop(1 if mine else 0, per, step, 0)
+
+    def keys_of(chunk):
+        row = jnp.full((1, LANES), -1, jnp.int32)
+        for part in range(chunks):
+            row = jnp.where(chunk == part, key_rows[part], row)
+        return row
+
+    def block(chunk):
+        return recv_u[pl.ds(chunk * per, per)].reshape(LANES, width)
+
+    def best_of(panel, panel_keys, queries, query_keys):
         scores = lax.dot_general(panel, queries, (((1,), (1,)), ((), ())), preferred_element_type=jnp.float32)
-        query_keys = jnp.full((1, LANES), -1, jnp.int32)
-        for part in range(chunks):
-            query_keys = jnp.where(chunk == part, key_rows[part], query_keys)
         first = query_keys & (-(1 << bits))
-        mask = (keys_column < query_keys) & (keys_column >= first)
-        answers[chunk] = jnp.max(jnp.where(mask, scores, -1.0), axis=0, keepdims=True)
-
-        def answer(k, carry, chunk=chunk):
+        mask = (panel_keys < query_keys) & (panel_keys >= first)
+        return jnp.max(jnp.where(mask, scores, -1.0), axis=0, keepdims=True)
+
+    last = order[1]
+    ready = order[2:] + order[:1]
+    for chunk in reversed(ready[:-1]):
+        await_units(chunk, chunk is order[-1])
+    await_units(order[0], False)
+    ready_rows = jnp.concatenate([block(c) for c in ready], axis=0)
+    ready_keys = jnp.concatenate([columns(keys_of(c)) for c in ready], axis=0)
+    partial = [best_of(ready_rows, ready_keys, block(c), keys_of(c)) for c in ready]
+    for index, found in enumerate(partial):
+        answers[ready[index]] = found
+    await_units(last, False)
+    last_rows, last_keys = block(last), keys_of(last)
+    last_column = columns(last_keys)
+
+    def answer_to(chunk, mine):
+        def step(k, carry):
             copy_answers(chunk * per + lax.rem(my_place + k, per)).start()
             return carry
-
-        lax.fori_loop(1 if index == chunks - 1 else 0, per, answer, 0)
+        lax.fori_loop(1 if mine else 0, per, step, 0)
+
+    def complete_answer(chunk, mine):
+        more = best_of(last_rows, last_column, block(chunk), keys_of(chunk))
+        answers[chunk] = jnp.maximum(answers[chunk], more)
+        answer_to(chunk, mine)
+
+    complete_answer(order[0], False)
+    here = best_of(last_rows, last_column, last_rows, last_keys)
+    answers[last] = jnp.maximum(here, best_of(ready_rows, ready_keys, last_rows, last_keys))
+    answer_to(last, False)
+    for chunk in order[2:]:
+        complete_answer(chunk, chunk is order[-1])
 
     returned[me] = answers[my_chunk]
+
+    def finish(d):
+        copy_keys(d).wait_send()
+        copy_units(d).wait_send()
+        copy_answers(d).wait_send()
+
+    others(finish)
     others(lambda d: await_from(d)(returned, a_send, a_recv))
     gathered = returned[...].reshape(devices, LANES)
     device_row = lax.broadcasted_iota(jnp.int32, (devices, rows), 0)
@@ -201,13 +238,6 @@
         precision=lax.Precision.HIGHEST, preferred_element_type=jnp.float32)
     want = position + offset
     out_ref[...] = jnp.sum(jnp.where(chunk_row == want, spread, 0.0), axis=0, keepdims=True)
-
-    def finish(d):
-        copy_keys(d).wait_send()
-        copy_units(d).wait_send()
-        copy_answers(d).wait_send()
-
-    others(finish)
 
 
 def kernel_body(shards, pairs, embeds, cluster, rank):
@@ -220,7 +250,7 @@
     vmem = pl.BlockSpec(memory_space=pltpu.VMEM)
     best = pl.pallas_call(
         functools.partial(kernel, pairs, sub, bits, log2(CL_OWN // pairs)),
-        out_shape=jax.ShapeDtypeStruct((1, rows), jnp.float32),
+        out_shape=pltpu.VMEM((1, rows), jnp.float32),
         in_specs=[pl.BlockSpec(memory_space=pl.ANY)] * 3,
         out_specs=vmem,
         scratch_shapes=[
@@ -275,7 +305,7 @@
         quarter = CL_OWN // pairs
         fits = (
             CL_OWN % pairs == 0 and quarter & (quarter - 1) == 0
-            and sub % 16 == 0 and LANES % sub == 0 and devices % (LANES // sub) == 0
+            and sub % 16 == 0 and LANES % sub == 0 and devices == 4 * (LANES // sub)
             and rows % LANES == 0 and width % LANES == 0
         )
         if fits:

time: 35.9 us -> 33.9 us (0.944)
  Pallas kernels: 34.5 us -> 33.2 us
  local copies, waits for them, and re-layouts: 1.22 us -> 0.56 us
    pallas_call x1, Pallas kernels: 34.5 us -> 33.2 us  [kernel_body(): pl.pallas_call(functools.partial(kernel, pairs, sub, bits, log2(CL_OWN //...]
    unnamed x3 -> x1, local copies, waits for them, and re-layouts: 1.22 us -> 0.56 us
where the time goes in v3:
time: 33.9 us; the launch traced here: 33.7 us
  Pallas kernels  33.2 us (98%)
  local copies, waits for them, and re-layouts  0.56 us (2%)
    pallas_call x1, Pallas kernels, kernel_body(): pl.pallas_call(functools.partial(kernel, pairs, sub, bits, log2(CL_OWN //...  33.2 us

profile of v3, /device:TPU:0, one launch (start us, length us, event | category | flops | bytes accessed | tf_op | source)
XLA Modules:
  0.0 33.7 jit_solution(14538599513848123245)
XLA Ops:
  0.0 33.2 %shard_map.37 = f32[1,256]{1,0:T(1,128)S(1)} custom-call(f32[256,768]{1,0:T(8,128)} %embeds_in.1, s32[1,256]{1,0:T(1,128)} %bitcast.4, s32[1,256]{1,0:T(1,128)} %bitcast.5), custom_call_target="tpu_custom_call" | custom-call | tf_op jit(solution)/shard_map/pallas_call | solution.py:251
  33.2 0.6 %copy.5 = f32[256]{0:T(256)} copy(f32[256]{0:T(256)S(1)} %bitcast.3) | data formatting | bytes 2048
